TPU v7x, 256 devices: a whole 4x4x8 slice. The times are simulated.
256 devices in a mesh: sec: 8 (over z_lo, core), ctx: 32 (over z_hi, x, y).
Axes of the slice: x: 4, y: 4, z: 8 (z_hi: 2, z_lo: 4; z = z_hi * 4 + z_lo), core: 2. Of those that a mesh axis runs over, the one named last changes fastest.
Arguments:
- q_frames: bfloat16 [8, 512, 8, 3584], P('sec', 'ctx'), may hold values from -8 to 8
- k_frames: bfloat16 [8, 512, 8, 512], P('sec', 'ctx'), may hold values from -8 to 8
- v_frames: bfloat16 [8, 512, 8, 512], P('sec', 'ctx'), may hold values from -6 to 6
- video_frames: int32 [8], replicated, may hold values from 256 to 512, as said below
- frame_section: int32 [8, 512], P('sec', 'ctx'), may hold values from 0 to 7, as said below
- frame_offset: int32 [8, 512], P('sec', 'ctx'), may hold values from 0 to 4088, as said below
Outputs:
- attention_out: bfloat16 [8, 4096, 3584], P('sec', 'ctx')
Inputs may be any that keep to these rules, and one draw needn't show every extreme that they name: `video_frames`: at least one section's video fills all 512 slots. `frame_section`: every device holds exactly 2 frame slots for each section. `frame_offset`: A multiple of 8; it falls in the 128 positions of the section's device whose ctx index equals that of the slot's device; the slots of one section cover its positions once. Slots at positions of frames beyond the video's length are not part of it.
All inputs are finite; a program needn't handle non-finite values.
Results may differ from a plain program's by a relative error of at most 0.006.
Values may be sent and summed in bfloat16 or wider, within the bound.
No kernel may reach another device: no remote copies, remote signals or barrier semaphores. Data moves between devices by JAX's collectives and lax.ppermute only.
A program may use at most 128 MiB of HBM per device.

v0:
```python
import math
import jax
import jax.numpy as jnp
from jax import lax
from jax.sharding import PartitionSpec as P

HEAD_DIM = 128
floor_score = -1e30


def source_slots(target_slot):
    slot_count = target_slot.shape[0]
    slot_ids = jnp.arange(slot_count, dtype=jnp.int32)
    matches = (target_slot[:, None] == slot_ids[None, :]).astype(jnp.int32)
    return jnp.sum(slot_ids[:, None] * matches, axis=0)


def make_absorb(query_sets, live_len, kv_heads, head_dim, score_scale):

    def absorb(carry, kv_piece, piece_start):
        key_block, value_block = kv_piece
        key_count = key_block.shape[0]
        key_pos = jnp.arange(key_count, dtype=jnp.int32)
        key_rows = key_block.reshape(key_count, kv_heads, head_dim)
        value_rows = value_block.reshape(key_count, kv_heads, head_dim)
        result = []
        for (queries, first_pos), carry_state in zip(query_sets, carry):
            row_count = queries.shape[0]
            active = (
                (piece_start <= first_pos + row_count - 1)
                & (piece_start < live_len)
                & (first_pos < live_len)
            )

            def advance(old_state, queries=queries, first_pos=first_pos, row_count=row_count):
                run_max, weight_sum, accumulated = old_state
                query_pos = first_pos + jnp.arange(row_count, dtype=jnp.int32)
                scores = (
                    jnp.einsum(
                        "rkgd,nkd->kgrn", queries, key_rows, preferred_element_type=jnp.float32
                    )
                    * score_scale
                )
                visible = (key_pos[None, :] <= query_pos[:, None]) & (key_pos[None, :] < live_len)
                masked = jnp.where(visible, scores, floor_score)
                new_max = jnp.maximum(run_max, jnp.max(masked, axis=-1))
                weights = jnp.where(visible, jnp.exp(scores - new_max[..., None]), 0.0)
                weight_sum = jnp.sum(weights, axis=-1)
                mixed = jnp.einsum(
                    "kgrn,nkd->rkgd",
                    weights.astype(jnp.bfloat16),
                    value_rows,
                    preferred_element_type=jnp.float32,
                )
                accumulated = mixed
                return (new_max, weight_sum, accumulated)

            result.append(lax.cond(active, advance, lambda unchanged: unchanged, carry_state))
        return tuple(result)

    return absorb


def finish(carry_state, first_pos, row_count, live_len):
    run_max, weight_sum, accumulated = carry_state
    query_pos = first_pos + jnp.arange(row_count, dtype=jnp.int32)
    is_live = query_pos < live_len
    safe_sum = jnp.where(is_live[None, None, :], weight_sum, 1.0)
    mixed = accumulated / jnp.transpose(safe_sum, (2, 0, 1))[..., None]
    mixed = mixed.reshape(row_count, -1)
    return jnp.where(is_live[:, None], mixed, 0.0).astype(jnp.bfloat16)


def local(q_frames, k_frames, v_frames, video_frames, frame_section, frame_offset):
    sections = lax.axis_size("sec")
    frames_dev = q_frames.shape[1]
    frame_len = q_frames.shape[2]
    per_section = frames_dev // sections
    kv_width = k_frames.shape[3]
    q_width = q_frames.shape[3]
    head_dim = HEAD_DIM
    kv_heads = kv_width // head_dim
    group_size = q_width // kv_width
    my_section = lax.axis_index("sec")
    my_place = lax.axis_index("ctx")
    section_of = frame_section[0]
    offsets = frame_offset[0]
    slot_ids = jnp.arange(frames_dev, dtype=jnp.int32)
    earlier = (section_of[:, None] == section_of[None, :]) & (slot_ids[None, :] < slot_ids[:, None])
    rank_in = jnp.sum(earlier.astype(jnp.int32), axis=1)
    order = source_slots(section_of * per_section + rank_in)
    send_q = jnp.take(q_frames[0], order, axis=0).reshape(sections, per_section, frame_len, q_width)
    send_k = jnp.take(k_frames[0], order, axis=0).reshape(
        sections, per_section, frame_len, kv_width
    )
    send_v = jnp.take(v_frames[0], order, axis=0).reshape(
        sections, per_section, frame_len, kv_width
    )
    send_off = jnp.take(offsets, order, axis=0).reshape(sections, per_section)
    got_q, got_k, got_v, got_off = (
        lax.all_to_all(send_q, "sec", split_axis=0, concat_axis=0, tiled=True),
        lax.all_to_all(send_k, "sec", split_axis=0, concat_axis=0, tiled=True),
        lax.all_to_all(send_v, "sec", split_axis=0, concat_axis=0, tiled=True),
        lax.all_to_all(send_off, "sec", split_axis=0, concat_axis=0, tiled=True),
    )
    local_slot = got_off.reshape(frames_dev) // frame_len - my_place * frames_dev
    placing = source_slots(local_slot)
    row_count = frames_dev * frame_len
    local_q = jnp.take(got_q.reshape(frames_dev, frame_len, q_width), placing, axis=0).reshape(
        row_count, q_width
    )
    local_k = jnp.take(got_k.reshape(frames_dev, frame_len, kv_width), placing, axis=0).reshape(
        row_count, kv_width
    )
    local_v = jnp.take(got_v.reshape(frames_dev, frame_len, kv_width), placing, axis=0).reshape(
        row_count, kv_width
    )
    live_len = video_frames[my_section] * frame_len
    half_rows = row_count // 2
    base_pos = my_place * row_count
    lead_q = local_q[:half_rows]
    tail_q = local_q[half_rows:]
    first_set = (lead_q, base_pos)
    second_set = (tail_q, base_pos + half_rows)
    query_sets = []
    for queries, first_pos in (first_set, second_set):
        query_sets.append((queries.reshape(half_rows, kv_heads, group_size, head_dim), first_pos))
    empty_state = (
        jnp.full((kv_heads, group_size, half_rows), floor_score, jnp.float32),
        jnp.zeros((kv_heads, group_size, half_rows), jnp.float32),
        jnp.zeros((half_rows, kv_heads, group_size, head_dim), jnp.float32),
    )
    absorb = make_absorb(query_sets, live_len, kv_heads, head_dim, 1.0 / math.sqrt(head_dim))
    states = absorb(
        (empty_state, empty_state),
        (
            lax.all_gather(local_k, "ctx", axis=0, tiled=True),
            lax.all_gather(local_v, "ctx", axis=0, tiled=True),
        ),
        jnp.int32(0),
    )
    first_out = finish(states[0], first_set[1], half_rows, live_len)
    second_out = finish(states[1], second_set[1], half_rows, live_len)
    return jnp.concatenate([first_out, second_out], axis=0)[None]


def solution(mesh):
    placed = (
        P("sec", "ctx", None, None),
        P("sec", "ctx", None, None),
        P("sec", "ctx", None, None),
        P(),
        P("sec", "ctx"),
        P("sec", "ctx"),
    )
    return jax.shard_map(
        local, mesh=mesh, in_specs=placed, out_specs=P("sec", "ctx", None), check_vma=False
    )
```

profile of v0, /device:TPU:32, one launch (start us, length us, event | category | flops | bytes accessed | tf_op | source)
XLA Modules:
  0.0 373.2 jit_solution(9911036601801687669)
XLA Ops:
  6.5 0.9 convert_reduce_fusion
  7.5 0.7 multiply_add_fusion
  8.3 1.3 gather_fusion
  9.7 0.6 and_select_fusion
  10.3 6.0 %all-to-all-start.1 = ((s32[8,1,2]{2,1,0:T(1,128)}), s32[8,1,2]{2,1,0:T(1,128)S(1)}, u32[]{:S(2)}, u32[]{:S(2)}) async-start(s32[8,1,2]{2,1,0:T(1,128)} %bitcast.13), calls=%async_computation.1 | async-start | bytes 8192 | tf_op jit(solution)/shard_map/all_to_all | solution.py:104
  16.4 1.5 gather_fusion.5
  17.8 1.5 gather_fusion.3
  19.3 0.8 broadcast_select_fusion.2
  20.4 4.8 %all-to-all-start.2 = ((bf16[8,2,8,512]{3,2,1,0:T(8,128)(2,1)}), bf16[8,2,8,512]{3,2,1,0:T(8,128)(2,1)S(1)}, u32[]{:S(2)}, u32[]{:S(2)}) async-start(bf16[8,2,8,512]{3,2,1,0:T(8,128)(2,1)} %bitcast.18), calls=%async_computation.2 | async-start | bytes 262144 | tf_op jit(solution)/shard_map/all_to_all | solution.py:102
  25.2 0.6 broadcast.297
  25.8 0.6 reduce.3
  26.6 4.3 %all-to-all-done.2 = bf16[8,2,8,512]{3,2,1,0:T(8,128)(2,1)S(1)} async-done(((bf16[8,2,8,512]{3,2,1,0:T(8,128)(2,1)}), bf16[8,2,8,512]{3,2,1,0:T(8,128)(2,1)S(1)}, u32[]{:S(2)}, u32[]{:S(2)}) %all-to-all-start.2) | async-done | bytes 131104 | tf_op jit(solution)/shard_map/all_to_all | solution.py:102
  30.9 4.4 %all-to-all-start.3 = ((bf16[8,2,8,512]{3,2,1,0:T(8,128)(2,1)}), bf16[8,2,8,512]{3,2,1,0:T(8,128)(2,1)S(1)}, u32[]{:S(2)}, u32[]{:S(2)}) async-start(bf16[8,2,8,512]{3,2,1,0:T(8,128)(2,1)} %bitcast.23), calls=%async_computation.3 | async-start | bytes 262144 | tf_op jit(solution)/shard_map/all_to_all | solution.py:103
  35.3 0.6 gather_fusion.4
  35.8 5.1 %all-to-all-done.3 = bf16[8,2,8,512]{3,2,1,0:T(8,128)(2,1)S(1)} async-done(((bf16[8,2,8,512]{3,2,1,0:T(8,128)(2,1)}), bf16[8,2,8,512]{3,2,1,0:T(8,128)(2,1)S(1)}, u32[]{:S(2)}, u32[]{:S(2)}) %all-to-all-start.3) | async-done | bytes 131104 | tf_op jit(solution)/shard_map/all_to_all | solution.py:103
  41.0 0.6 gather_fusion.6
  41.5 0.8 select_bitcast_fusion
  42.4 0.7 all-gather.3.cloned.1.call-update
  43.1 0.6 gather_fusion.1
  43.7 1.1 broadcast_select_fusion.1
  44.8 4.6 %all-to-all-start = ((bf16[8,2,8,3584]{3,2,1,0:T(8,128)(2,1)}), bf16[8,2,8,3584]{3,2,1,0:T(8,128)(2,1)S(1)}, u32[]{:S(2)}, u32[]{:S(2)}) async-start(bf16[8,2,8,3584]{3,2,1,0:T(8,128)(2,1)} %bitcast.15), calls=%async_computation | async-start | bytes 1835008 | tf_op jit(solution)/shard_map/all_to_all | solution.py:101
  49.4 1.3 dynamic_slice.3
  51.3 20.2 %all-to-all-done = bf16[8,2,8,3584]{3,2,1,0:T(8,128)(2,1)S(1)} async-done(((bf16[8,2,8,3584]{3,2,1,0:T(8,128)(2,1)}), bf16[8,2,8,3584]{3,2,1,0:T(8,128)(2,1)S(1)}, u32[]{:S(2)}, u32[]{:S(2)}) %all-to-all-start) | async-done | bytes 917536 | tf_op jit(solution)/shard_map/all_to_all | solution.py:101
  71.5 0.6 gather_fusion.2
  72.2 1.1 broadcast_select_fusion
  73.2 83.6 %all-gather.5.cloned.1.call-done = bf16[4096,512]{1,0:T(8,128)(2,1)} async-done(((bf16[128,512]{1,0:T(8,128)(2,1)}), bf16[4096,512]{1,0:T(8,128)(2,1)}) %all-gather.5.cloned.1.call-update) | async-done | bytes 4194320 | tf_op jit(solution)/shard_map/all_gather | solution.py:138
  156.8 6.4 %copy.42 = bf16[4096,512]{0,1:T(8,128)(2,1)} copy(bf16[4096,512]{1,0:T(8,128)(2,1)} %all-gather.5.cloned.1.call-done) | data formatting | bytes 8388608 | tf_op jit(solution)/shard_map/all_gather | solution.py:138
  163.2 102.9 %all-gather.3.cloned.1.call-done = bf16[4096,512]{1,0:T(8,128)(2,1)} async-done(((bf16[128,512]{1,0:T(8,128)(2,1)}), bf16[4096,512]{1,0:T(8,128)(2,1)}) %all-gather.3.cloned.1.call-update) | async-done | bytes 4194320 | tf_op jit(solution)/shard_map/all_gather | solution.py:137
  266.1 6.4 %copy.41 = bf16[4096,512]{0,1:T(8,128)(2,1)} copy(bf16[4096,512]{1,0:T(8,128)(2,1)} %all-gather.3.cloned.1.call-done) | data formatting | bytes 8388608 | tf_op jit(solution)/shard_map/all_gather | solution.py:137
  272.5 42.3 %conditional.2 = (f32[4,7,64]{2,1,0:T(8,128)S(1)}, f32[64,4,7,128]{3,0,2,1:T(8,128)}) conditional(s32[]{:T(128)} %convert_element_type.23, () %tuple.23, (s32[4096]{0:T(1024)S(1)}, s32[]{:T(128)}, s32[]{:T(128)}, s32[4096]{0:T(1024)S(1)}, bf16[16,8,3584]{2,1,0:T(8,128)(2,1)}, /*index=5*/bf16[4096,4,128]{0,2,1:T(8,128)(2,1)}, ...), branch_computations={%region_3.0_spmd, %region_4.9_spmd} | conditional | flops 3839363328 | bytes 117590584 | solution.py:58
  272.8 1.1 slice.8
  273.9 0.6 reshape.200
  274.5 13.9 %fusion = (f32[4,7,64]{2,1,0:T(8,128)S(1)}, f32[4,4096,64,7]{1,2,3,0:T(8,128)}) fusion(pred[64,4096]{1,0:T(8,128)(4,1)S(1)} %compare_and_fusion, bf16[64,4,7,128]{3,2,1,0:T(8,128)(2,1)S(1)} %reshape.200, bf16[4096,4,128]{0,2,1:T(8,128)(2,1)} %get-tuple-element.106), kind=kOutput, calls=%fused_computation.9 | convolution fusion | flops 1901066496 | bytes 34282496 | tf_op jit(solution)/shard_map/cond/branch_1_fun/rkgd,nkd->kgrn/dot_general | solution.py:39
  288.4 12.9 %fusion.11 = f32[64,4,7,128]{3,0,2,1:T(8,128)} fusion(bf16[4096,4,128]{0,2,1:T(8,128)(2,1)S(1)} %copy-done.2, f32[4,4096,64,7]{1,2,3,0:T(8,128)} %get-tuple-element.116, f32[4,7,64]{2,1,0:T(8,128)S(1)} %broadcast_maximum_fusion, pred[64,4096]{1,0:T(8,128)(4,1)S(1)} %compare_and_fusion), kind=kOutput, calls=%fused_computation.19 | convolution fusion | flops 1908408320 | bytes 34741248 | tf_op jit(solution)/shard_map/cond/branch_1_fun/kgrn,nkd->rkgd/dot_general | solution.py:49
  301.3 13.6 %fusion.4 = f32[4,7,64]{2,1,0:T(8,128)S(1)} fusion(f32[4,4096,64,7]{1,2,3,0:T(8,128)} %get-tuple-element.116, f32[4,7,64]{2,1,0:T(8,128)S(1)} %broadcast_maximum_fusion, pred[64,4096]{1,0:T(8,128)(4,1)S(1)} %compare_and_fusion), kind=kLoop, calls=%fused_computation.13 | loop fusion | flops 29358336 | bytes 29636608 | tf_op jit(solution)/shard_map/cond/branch_1_fun/reduce_sum | solution.py:48
  314.9 1.5 broadcast_divide_fusion.1
  316.7 0.5 reshape.226
  317.2 0.9 select_convert_fusion.1
  318.1 42.9 %conditional.3 = (f32[4,7,64]{2,1,0:T(8,128)}, f32[64,4,7,128]{3,0,2,1:T(8,128)}) conditional(s32[]{:T(128)} %convert_element_type.26, () %tuple.25, (s32[4096]{0:T(1024)S(1)}, s32[]{:T(128)}, s32[]{:T(128)}, s32[4096]{0:T(1024)S(1)}, bf16[16,8,3584]{2,1,0:T(8,128)(2,1)}, /*index=5*/bf16[4096,4,128]{0,2,1:T(8,128)(2,1)}, ...), branch_computations={%region_7.10_spmd, %region_8.13_spmd} | conditional | flops 3839363328 | bytes 117590584 | solution.py:58
  318.4 1.1 slice.9
  319.5 0.6 reshape.201
  320.0 13.9 %fusion.19 = (f32[4,7,64]{2,1,0:T(8,128)S(1)}, f32[4,4096,64,7]{1,2,3,0:T(8,128)}) fusion(pred[64,4096]{1,0:T(8,128)(4,1)S(1)} %compare_and_fusion.1, bf16[64,4,7,128]{3,2,1,0:T(8,128)(2,1)S(1)} %reshape.201, bf16[4096,4,128]{0,2,1:T(8,128)(2,1)} %get-tuple-element.113), kind=kOutput, calls=%fused_computation.29 | convolution fusion | flops 1901066496 | bytes 34282496 | tf_op jit(solution)/shard_map/cond/branch_1_fun/rkgd,nkd->kgrn/dot_general | solution.py:39
  334.0 12.9 %fusion.30 = f32[64,4,7,128]{3,0,2,1:T(8,128)} fusion(bf16[4096,4,128]{0,2,1:T(8,128)(2,1)S(1)} %copy-done.3, f32[4,4096,64,7]{1,2,3,0:T(8,128)} %get-tuple-element.118, f32[4,7,64]{2,1,0:T(8,128)S(1)} %broadcast_maximum_fusion.1, pred[64,4096]{1,0:T(8,128)(4,1)S(1)} %compare_and_fusion.1), kind=kOutput, calls=%fused_computation.39 | convolution fusion | flops 1908408320 | bytes 34741248 | tf_op jit(solution)/shard_map/cond/branch_1_fun/kgrn,nkd->rkgd/dot_general | solution.py:49
  346.9 14.2 %fusion.23 = f32[4,7,64]{2,1,0:T(8,128)} fusion(f32[4,4096,64,7]{1,2,3,0:T(8,128)} %get-tuple-element.118, f32[4,7,64]{2,1,0:T(8,128)S(1)} %broadcast_maximum_fusion.1, pred[64,4096]{1,0:T(8,128)(4,1)S(1)} %compare_and_fusion.1), kind=kLoop, calls=%fused_computation.33 | loop fusion | flops 29358336 | bytes 29636608 | tf_op jit(solution)/shard_map/cond/branch_1_fun/reduce_sum | solution.py:48
  361.1 0.8 select_bitcast_fusion.2
  361.9 1.5 broadcast_divide_fusion
  363.7 0.5 reshape.227
  364.3 2.0 maximum_bitcast_fusion
  (41 shorter events, 2.2 us)
Async XLA Ops:
  6.5 36.6 %copy-start = (bf16[1,16,8,3584]{3,2,1,0:T(8,128)(2,1)S(1)}, bf16[1,16,8,3584]{3,2,1,0:T(8,128)(2,1)}, u32[]{:S(2)}) copy-start(bf16[1,16,8,3584]{3,2,1,0:T(8,128)(2,1)} %param.14) | copy-start | bytes 2752516
  10.3 10.1 %all-to-all-start.1 = ((s32[8,1,2]{2,1,0:T(1,128)}), s32[8,1,2]{2,1,0:T(1,128)S(1)}, u32[]{:S(2)}, u32[]{:S(2)}) async-start(s32[8,1,2]{2,1,0:T(1,128)} %bitcast.13), calls=%async_computation.1 | async-start | bytes 8192 | tf_op jit(solution)/shard_map/all_to_all | solution.py:104
  20.4 10.4 %all-to-all-start.2 = ((bf16[8,2,8,512]{3,2,1,0:T(8,128)(2,1)}), bf16[8,2,8,512]{3,2,1,0:T(8,128)(2,1)S(1)}, u32[]{:S(2)}, u32[]{:S(2)}) async-start(bf16[8,2,8,512]{3,2,1,0:T(8,128)(2,1)} %bitcast.18), calls=%async_computation.2 | async-start | bytes 262144 | tf_op jit(solution)/shard_map/all_to_all | solution.py:102
  30.9 10.1 %all-to-all-start.3 = ((bf16[8,2,8,512]{3,2,1,0:T(8,128)(2,1)}), bf16[8,2,8,512]{3,2,1,0:T(8,128)(2,1)S(1)}, u32[]{:S(2)}, u32[]{:S(2)}) async-start(bf16[8,2,8,512]{3,2,1,0:T(8,128)(2,1)} %bitcast.23), calls=%async_computation.3 | async-start | bytes 262144 | tf_op jit(solution)/shard_map/all_to_all | solution.py:103
  35.3 121.5 %all-gather.5.cloned.1.call-start = ((), (), s32[]{:S(2)}) async-start(), calls=%async_computation.5 | async-start | bytes 4325376 | tf_op jit(solution)/shard_map/all_gather | solution.py:138
  42.4 223.7 %all-gather.3.cloned.1.call-start = ((), (), s32[]{:S(2)}) async-start(), calls=%async_computation.4 | async-start | bytes 4325376 | tf_op jit(solution)/shard_map/all_gather | solution.py:137
  44.8 26.7 %all-to-all-start = ((bf16[8,2,8,3584]{3,2,1,0:T(8,128)(2,1)}), bf16[8,2,8,3584]{3,2,1,0:T(8,128)(2,1)S(1)}, u32[]{:S(2)}, u32[]{:S(2)}) async-start(bf16[8,2,8,3584]{3,2,1,0:T(8,128)(2,1)} %bitcast.15), calls=%async_computation | async-start | bytes 1835008 | tf_op jit(solution)/shard_map/all_to_all | solution.py:101
  274.4 14.0 %copy-start.2 = (bf16[4096,4,128]{0,2,1:T(8,128)(2,1)S(1)}, bf16[4096,4,128]{0,2,1:T(8,128)(2,1)}, u32[]{:S(2)}) copy-start(bf16[4096,4,128]{0,2,1:T(8,128)(2,1)} %get-tuple-element.107) | copy-start | bytes 12582916 | tf_op jit(solution)/shard_map/cond
  320.0 14.0 %copy-start.3 = (bf16[4096,4,128]{0,2,1:T(8,128)(2,1)S(1)}, bf16[4096,4,128]{0,2,1:T(8,128)(2,1)}, u32[]{:S(2)}) copy-start(bf16[4096,4,128]{0,2,1:T(8,128)(2,1)} %get-tuple-element.114) | copy-start | bytes 12582916 | tf_op jit(solution)/shard_map/cond
  361.1 5.3 %copy-start.1 = (bf16[1,16,8,3584]{3,2,1,0:T(8,128)(2,1)S(1)}, bf16[1,16,8,3584]{3,2,1,0:T(8,128)(2,1)}, u32[]{:S(2)}) copy-start(bf16[1,16,8,3584]{3,2,1,0:T(8,128)(2,1)} %param.14) | copy-start | bytes 2752516
Sparse Core Ops, SparseCore 0:
  42.5 114.2 all-gather.4
  160.3 105.7 all-gather.2
where the time goes:
time: 374 us; the launch traced here: 373 us
  waiting for transfers between devices  217 us (58%)
  matrix products  53.7 us (14%)
  other arithmetic  41.9 us (11%)
  local copies, waits for them, and re-layouts  26.4 us (7%)
  starting transfers between devices  19.8 us (5%)
  between operations  14.2 us (4%)
    all_gather x1, waiting for transfers between devices, local(): lax.all_gather(local_k, 'ctx', axis=0, tiled=True)  103 us
    all_gather x1, waiting for transfers between devices, local(): lax.all_gather(local_v, 'ctx', axis=0, tiled=True)  83.6 us
    dot_general x2, matrix products, advance(): jnp.einsum('rkgd,nkd->kgrn', queries, key_rows, preferred_element_type=jn...  27.9 us
    reduce_sum x2, other arithmetic, advance(): weight_sum = jnp.sum(weights, axis=-1)  27.7 us
    dot_general x2, matrix products, advance(): jnp.einsum('kgrn,nkd->rkgd', weights.astype(jnp.bfloat16), value_rows, pr...  25.8 us
    all_to_all x1, waiting for transfers between devices, local(): lax.all_to_all(send_q, 'sec', split_axis=0, concat_axis=0, tiled=True)  20.2 us
  transfers between devices with their start and end apart: 6, of which 6 were waited for; matrix products, arithmetic and copies ran while one was open for 4% of the time, Pallas kernels for 0%

commit v1 on v0

--- a/solution.py
+++ b/solution.py
@@ -6,6 +6,13 @@
 
 HEAD_DIM = 128
 floor_score = -1e30
+
+
+def swapped_in(x, name, dim):
+    peers = lax.axis_size(name)
+    tiles = jnp.stack([x for _ in range(peers)])
+    tiles = lax.all_to_all(tiles, name, split_axis=0, concat_axis=0)
+    return jnp.concatenate(tiles, axis=dim)
 
 
 def source_slots(target_slot):
@@ -133,10 +140,7 @@
     absorb = make_absorb(query_sets, live_len, kv_heads, head_dim, 1.0 / math.sqrt(head_dim))
     states = absorb(
         (empty_state, empty_state),
-        (
-            lax.all_gather(local_k, "ctx", axis=0, tiled=True),
-            lax.all_gather(local_v, "ctx", axis=0, tiled=True),
-        ),
+        (swapped_in(local_k, "ctx", 0), lax.all_gather(local_v, "ctx", axis=0, tiled=True)),
         jnp.int32(0),
     )
     first_out = finish(states[0], first_set[1], half_rows, live_len)

time: 374 us -> 347 us (0.928)
  waiting for transfers between devices: 217 us -> 164 us
  starting transfers between devices: 19.8 us -> 31.2 us
  local copies, waits for them, and re-layouts: 26.4 us -> 37.1 us
    all_gather x1 -> x0, waiting for transfers between devices: 103 us -> none  [local(): lax.all_gather(local_k, 'ctx', axis=0, tiled=True)]
    all_gather x1, waiting for transfers between devices: 83.6 us -> 136 us  [local(): lax.all_gather(local_v, 'ctx', axis=0, tiled=True)]
    all_to_all x0 -> x1, starting transfers between devices: none -> 11.5 us  [swapped_in(): tiles = lax.all_to_all(tiles, name, split_axis=0, concat_axis=0)]
    another operation x0 -> x3, local copies, waits for them, and re-layouts: none -> 10.3 us  [the longest x1 7.32 us: absorb(): key_rows = key_block.reshape(key_count, kv_heads, head_dim)]
    all_to_all x0 -> x1, local copies, waits for them, and re-layouts: none -> 6.86 us  [swapped_in(): tiles = lax.all_to_all(tiles, name, split_axis=0, concat_axis=0)]
    all_gather x1 -> x0, local copies, waits for them, and re-layouts: 6.43 us -> none  [local(): lax.all_gather(local_k, 'ctx', axis=0, tiled=True)]
  transfers between devices with their start and end apart: 6 -> 6, of which waited for: 6 -> 5; matrix products, arithmetic and copies ran while one was open for 4% -> 6% of each run, Pallas kernels for 0% -> 0%
where the time goes in v1:
time: 347 us; the launch traced here: 343 us
  waiting for transfers between devices  164 us (47%)
  matrix products  53.7 us (15%)
  other arithmetic  41.9 us (12%)
  local copies, waits for them, and re-layouts  37.1 us (11%)
  starting transfers between devices  31.2 us (9%)
  between operations  14.2 us (4%)
    all_gather x1, waiting for transfers between devices, local(): lax.all_gather(local_v, 'ctx', axis=0, tiled=True)  136 us
    dot_general x2, matrix products, advance(): jnp.einsum('rkgd,nkd->kgrn', queries, key_rows, preferred_element_type=jn...  27.9 us
    reduce_sum x2, other arithmetic, advance(): weight_sum = jnp.sum(weights, axis=-1)  27.7 us
    dot_general x2, matrix products, advance(): jnp.einsum('kgrn,nkd->rkgd', weights.astype(jnp.bfloat16), value_rows, pr...  25.8 us
    all_to_all x1, waiting for transfers between devices, local(): lax.all_to_all(send_q, 'sec', split_axis=0, concat_axis=0, tiled=True)  17.8 us
    all_to_all x1, starting transfers between devices, swapped_in(): tiles = lax.all_to_all(tiles, name, split_axis=0, concat_axis=0)  11.5 us
    another operation x1, local copies, waits for them, and re-layouts, absorb(): key_rows = key_block.reshape(key_count, kv_heads, head_dim)  7.32 us
  transfers between devices with their start and end apart: 6, of which 5 were waited for; matrix products, arithmetic and copies ran while one was open for 6% of the time, Pallas kernels for 0%

profile of v1, /device:TPU:32, one launch (start us, length us, event | category | flops | bytes accessed | tf_op | source)
XLA Modules:
  0.0 342.6 jit_solution(9119488164202849220)
XLA Ops:
  6.5 0.9 convert_reduce_fusion
  7.5 0.7 multiply_add_fusion
  8.3 1.3 gather_fusion
  9.7 0.6 and_select_fusion
  10.3 6.0 %all-to-all-start.1 = ((s32[8,1,2]{2,1,0:T(1,128)}), s32[8,1,2]{2,1,0:T(1,128)S(1)}, u32[]{:S(2)}, u32[]{:S(2)}) async-start(s32[8,1,2]{2,1,0:T(1,128)} %bitcast.13), calls=%async_computation.1 | async-start | bytes 8192 | tf_op jit(solution)/shard_map/all_to_all | solution.py:111
  16.4 1.5 gather_fusion.5
  17.8 1.5 gather_fusion.3
  19.3 0.8 broadcast_select_fusion.2
  20.4 4.8 %all-to-all-start.2 = ((bf16[8,2,8,512]{3,2,1,0:T(8,128)(2,1)}), bf16[8,2,8,512]{3,2,1,0:T(8,128)(2,1)S(1)}, u32[]{:S(2)}, u32[]{:S(2)}) async-start(bf16[8,2,8,512]{3,2,1,0:T(8,128)(2,1)} %bitcast.18), calls=%async_computation.2 | async-start | bytes 262144 | tf_op jit(solution)/shard_map/all_to_all | solution.py:109
  25.2 0.6 gather_fusion.1
  25.8 5.1 %all-to-all-done.2 = bf16[8,2,8,512]{3,2,1,0:T(8,128)(2,1)S(1)} async-done(((bf16[8,2,8,512]{3,2,1,0:T(8,128)(2,1)}), bf16[8,2,8,512]{3,2,1,0:T(8,128)(2,1)S(1)}, u32[]{:S(2)}, u32[]{:S(2)}) %all-to-all-start.2) | async-done | bytes 131104 | tf_op jit(solution)/shard_map/all_to_all | solution.py:109
  30.9 4.4 %all-to-all-start.4 = ((bf16[8,2,8,512]{3,2,1,0:T(8,128)(2,1)}), bf16[8,2,8,512]{3,2,1,0:T(8,128)(2,1)S(1)}, u32[]{:S(2)}, u32[]{:S(2)}) async-start(bf16[8,2,8,512]{3,2,1,0:T(8,128)(2,1)} %bitcast.22), calls=%async_computation.4 | async-start | bytes 262144 | tf_op jit(solution)/shard_map/all_to_all | solution.py:110
  35.3 1.1 broadcast_select_fusion.1
  36.3 4.6 %all-to-all-done.4 = bf16[8,2,8,512]{3,2,1,0:T(8,128)(2,1)S(1)} async-done(((bf16[8,2,8,512]{3,2,1,0:T(8,128)(2,1)}), bf16[8,2,8,512]{3,2,1,0:T(8,128)(2,1)S(1)}, u32[]{:S(2)}, u32[]{:S(2)}) %all-to-all-start.4) | async-done | bytes 131104 | tf_op jit(solution)/shard_map/all_to_all | solution.py:110
  41.0 4.6 %all-to-all-start = ((bf16[8,2,8,3584]{3,2,1,0:T(8,128)(2,1)}), bf16[8,2,8,3584]{3,2,1,0:T(8,128)(2,1)S(1)}, u32[]{:S(2)}, u32[]{:S(2)}) async-start(bf16[8,2,8,3584]{3,2,1,0:T(8,128)(2,1)} %bitcast.15), calls=%async_computation | async-start | bytes 1835008 | tf_op jit(solution)/shard_map/all_to_all | solution.py:108
  45.5 0.6 broadcast.298
  46.1 0.6 reduce.3
  47.0 0.6 gather_fusion.4
  47.6 0.6 gather_fusion.6
  48.1 0.7 select_bitcast_fusion
  49.0 17.8 %all-to-all-done = bf16[8,2,8,3584]{3,2,1,0:T(8,128)(2,1)S(1)} async-done(((bf16[8,2,8,3584]{3,2,1,0:T(8,128)(2,1)}), bf16[8,2,8,3584]{3,2,1,0:T(8,128)(2,1)S(1)}, u32[]{:S(2)}, u32[]{:S(2)}) %all-to-all-start) | async-done | bytes 917536 | tf_op jit(solution)/shard_map/all_to_all | solution.py:108
  66.8 2.9 stack.3
  69.7 11.5 %all-to-all-start.3 = ((bf16[32,128,512]{1,2,0:T(8,128)(2,1)}), bf16[32,128,512]{1,2,0:T(8,128)(2,1)}, u32[]{:S(2)}, u32[]{:S(2)}) async-start(bf16[32,128,512]{1,2,0:T(8,128)(2,1)} %stack.3), calls=%async_computation.3 | async-start | bytes 8388608 | tf_op jit(solution)/shard_map/all_to_all | solution.py:14
  81.2 1.2 dynamic_slice.3
  83.1 0.6 gather_fusion.2
  83.7 1.1 broadcast_select_fusion
  84.8 136.3 %all-gather.2.cloned.1.call-done = bf16[4096,512]{1,0:T(8,128)(2,1)} async-done(((bf16[128,512]{1,0:T(8,128)(2,1)}), bf16[4096,512]{1,0:T(8,128)(2,1)}) %all-gather.2.cloned.1.call-update) | async-done | bytes 4194320 | tf_op jit(solution)/shard_map/all_gather | solution.py:143
  221.1 6.4 %copy.45 = bf16[4096,512]{0,1:T(8,128)(2,1)} copy(bf16[4096,512]{1,0:T(8,128)(2,1)} %all-gather.2.cloned.1.call-done) | data formatting | bytes 8388608 | tf_op jit(solution)/shard_map/all_gather | solution.py:143
  227.5 6.9 %copy.44 = bf16[32,128,512]{1,0,2:T(8,128)(2,1)} copy(bf16[32,128,512]{1,2,0:T(8,128)(2,1)} %all-to-all-done.3) | data formatting | bytes 8388608 | tf_op jit(solution)/shard_map/all_to_all | solution.py:14
  234.4 7.3 %reshape_reshape.3 = bf16[4096,4,128]{0,2,1:T(8,128)(2,1)} reshape(bf16[32,128,512]{1,0,2:T(8,128)(2,1)} %copy.44) | data formatting | bytes 8388608 | tf_op jit(solution)/shard_map/reshape;reshape | solution.py:31
  241.7 42.6 %conditional.2 = (f32[4,7,64]{2,1,0:T(8,128)S(1)}, f32[64,4,7,128]{3,0,2,1:T(8,128)}) conditional(s32[]{:T(128)} %convert_element_type.23, () %tuple.23, (s32[4096]{0:T(1024)S(1)}, s32[]{:T(128)}, s32[]{:T(128)}, s32[4096]{0:T(1024)S(1)}, bf16[16,8,3584]{2,1,0:T(8,128)(2,1)}, /*index=5*/bf16[4096,4,128]{0,2,1:T(8,128)(2,1)}, ...), branch_computations={%region_3.0_spmd, %region_4.9_spmd} | conditional | flops 3839363328 | bytes 117590584 | solution.py:65
  242.2 1.1 slice.8
  243.2 0.6 reshape.198
  243.8 14.0 %fusion = (f32[4,7,64]{2,1,0:T(8,128)S(1)}, f32[4,4096,64,7]{1,2,3,0:T(8,128)}) fusion(pred[64,4096]{1,0:T(8,128)(4,1)S(1)} %compare_and_fusion, bf16[64,4,7,128]{3,2,1,0:T(8,128)(2,1)S(1)} %reshape.198, bf16[4096,4,128]{0,2,1:T(8,128)(2,1)} %get-tuple-element.106), kind=kOutput, calls=%fused_computation.9 | convolution fusion | flops 1901066496 | bytes 34282496 | tf_op jit(solution)/shard_map/cond/branch_1_fun/rkgd,nkd->kgrn/dot_general | solution.py:46
  257.8 12.9 %fusion.11 = f32[64,4,7,128]{3,0,2,1:T(8,128)} fusion(bf16[4096,4,128]{0,2,1:T(8,128)(2,1)S(1)} %copy-done.2, f32[4,4096,64,7]{1,2,3,0:T(8,128)} %get-tuple-element.116, f32[4,7,64]{2,1,0:T(8,128)S(1)} %broadcast_maximum_fusion, pred[64,4096]{1,0:T(8,128)(4,1)S(1)} %compare_and_fusion), kind=kOutput, calls=%fused_computation.19 | convolution fusion | flops 1908408320 | bytes 34741248 | tf_op jit(solution)/shard_map/cond/branch_1_fun/kgrn,nkd->rkgd/dot_general | solution.py:56
  270.7 13.6 %fusion.4 = f32[4,7,64]{2,1,0:T(8,128)S(1)} fusion(f32[4,4096,64,7]{1,2,3,0:T(8,128)} %get-tuple-element.116, f32[4,7,64]{2,1,0:T(8,128)S(1)} %broadcast_maximum_fusion, pred[64,4096]{1,0:T(8,128)(4,1)S(1)} %compare_and_fusion), kind=kLoop, calls=%fused_computation.13 | loop fusion | flops 29358336 | bytes 29636608 | tf_op jit(solution)/shard_map/cond/branch_1_fun/reduce_sum | solution.py:55
  284.3 1.5 broadcast_divide_fusion.1
  286.1 0.5 reshape.220
  286.6 0.9 select_convert_fusion.1
  287.5 42.9 %conditional.3 = (f32[4,7,64]{2,1,0:T(8,128)}, f32[64,4,7,128]{3,0,2,1:T(8,128)}) conditional(s32[]{:T(128)} %convert_element_type.26, () %tuple.25, (s32[4096]{0:T(1024)S(1)}, s32[]{:T(128)}, s32[]{:T(128)}, s32[4096]{0:T(1024)S(1)}, bf16[16,8,3584]{2,1,0:T(8,128)(2,1)}, /*index=5*/bf16[4096,4,128]{0,2,1:T(8,128)(2,1)}, ...), branch_computations={%region_7.10_spmd, %region_8.13_spmd} | conditional | flops 3839363328 | bytes 117590584 | solution.py:65
  287.8 1.1 slice.9
  288.8 0.6 reshape.199
  289.4 14.0 %fusion.19 = (f32[4,7,64]{2,1,0:T(8,128)S(1)}, f32[4,4096,64,7]{1,2,3,0:T(8,128)}) fusion(pred[64,4096]{1,0:T(8,128)(4,1)S(1)} %compare_and_fusion.1, bf16[64,4,7,128]{3,2,1,0:T(8,128)(2,1)S(1)} %reshape.199, bf16[4096,4,128]{0,2,1:T(8,128)(2,1)} %get-tuple-element.113), kind=kOutput, calls=%fused_computation.29 | convolution fusion | flops 1901066496 | bytes 34282496 | tf_op jit(solution)/shard_map/cond/branch_1_fun/rkgd,nkd->kgrn/dot_general | solution.py:46
  303.4 12.9 %fusion.30 = f32[64,4,7,128]{3,0,2,1:T(8,128)} fusion(bf16[4096,4,128]{0,2,1:T(8,128)(2,1)S(1)} %copy-done.3, f32[4,4096,64,7]{1,2,3,0:T(8,128)} %get-tuple-element.118, f32[4,7,64]{2,1,0:T(8,128)S(1)} %broadcast_maximum_fusion.1, pred[64,4096]{1,0:T(8,128)(4,1)S(1)} %compare_and_fusion.1), kind=kOutput, calls=%fused_computation.39 | convolution fusion | flops 1908408320 | bytes 34741248 | tf_op jit(solution)/shard_map/cond/branch_1_fun/kgrn,nkd->rkgd/dot_general | solution.py:56
  316.3 14.2 %fusion.23 = f32[4,7,64]{2,1,0:T(8,128)} fusion(f32[4,4096,64,7]{1,2,3,0:T(8,128)} %get-tuple-element.118, f32[4,7,64]{2,1,0:T(8,128)S(1)} %broadcast_maximum_fusion.1, pred[64,4096]{1,0:T(8,128)(4,1)S(1)} %compare_and_fusion.1), kind=kLoop, calls=%fused_computation.33 | loop fusion | flops 29358336 | bytes 29636608 | tf_op jit(solution)/shard_map/cond/branch_1_fun/reduce_sum | solution.py:55
  330.5 0.8 select_bitcast_fusion.2
  331.3 1.5 broadcast_divide_fusion
  333.7 2.0 maximum_bitcast_fusion
  (43 shorter events, 2.8 us)
Async XLA Ops:
  6.5 18.7 %copy-start = (bf16[1,16,8,3584]{3,2,1,0:T(8,128)(2,1)S(1)}, bf16[1,16,8,3584]{3,2,1,0:T(8,128)(2,1)}, u32[]{:S(2)}) copy-start(bf16[1,16,8,3584]{3,2,1,0:T(8,128)(2,1)} %param.14) | copy-start | bytes 2752516
  10.3 10.1 %all-to-all-start.1 = ((s32[8,1,2]{2,1,0:T(1,128)}), s32[8,1,2]{2,1,0:T(1,128)S(1)}, u32[]{:S(2)}, u32[]{:S(2)}) async-start(s32[8,1,2]{2,1,0:T(1,128)} %bitcast.13), calls=%async_computation.1 | async-start | bytes 8192 | tf_op jit(solution)/shard_map/all_to_all | solution.py:111
  20.4 10.4 %all-to-all-start.2 = ((bf16[8,2,8,512]{3,2,1,0:T(8,128)(2,1)}), bf16[8,2,8,512]{3,2,1,0:T(8,128)(2,1)S(1)}, u32[]{:S(2)}, u32[]{:S(2)}) async-start(bf16[8,2,8,512]{3,2,1,0:T(8,128)(2,1)} %bitcast.18), calls=%async_computation.2 | async-start | bytes 262144 | tf_op jit(solution)/shard_map/all_to_all | solution.py:109
  30.9 10.1 %all-to-all-start.4 = ((bf16[8,2,8,512]{3,2,1,0:T(8,128)(2,1)}), bf16[8,2,8,512]{3,2,1,0:T(8,128)(2,1)S(1)}, u32[]{:S(2)}, u32[]{:S(2)}) async-start(bf16[8,2,8,512]{3,2,1,0:T(8,128)(2,1)} %bitcast.22), calls=%async_computation.4 | async-start | bytes 262144 | tf_op jit(solution)/shard_map/all_to_all | solution.py:110
  41.0 25.8 %all-to-all-start = ((bf16[8,2,8,3584]{3,2,1,0:T(8,128)(2,1)}), bf16[8,2,8,3584]{3,2,1,0:T(8,128)(2,1)S(1)}, u32[]{:S(2)}, u32[]{:S(2)}) async-start(bf16[8,2,8,3584]{3,2,1,0:T(8,128)(2,1)} %bitcast.15), calls=%async_computation | async-start | bytes 1835008 | tf_op jit(solution)/shard_map/all_to_all | solution.py:108
  45.5 175.6 %all-gather.2.cloned.1.call-start = ((), (), s32[]{:S(2)}) async-start(), calls=%async_computation.5 | async-start | bytes 4325376 | tf_op jit(solution)/shard_map/all_gather | solution.py:143
  69.7 157.8 %all-to-all-start.3 = ((bf16[32,128,512]{1,2,0:T(8,128)(2,1)}), bf16[32,128,512]{1,2,0:T(8,128)(2,1)}, u32[]{:S(2)}, u32[]{:S(2)}) async-start(bf16[32,128,512]{1,2,0:T(8,128)(2,1)} %stack.3), calls=%async_computation.3 | async-start | bytes 8388608 | tf_op jit(solution)/shard_map/all_to_all | solution.py:14
  243.8 14.0 %copy-start.2 = (bf16[4096,4,128]{0,2,1:T(8,128)(2,1)S(1)}, bf16[4096,4,128]{0,2,1:T(8,128)(2,1)}, u32[]{:S(2)}) copy-start(bf16[4096,4,128]{0,2,1:T(8,128)(2,1)} %get-tuple-element.107) | copy-start | bytes 12582916 | tf_op jit(solution)/shard_map/cond
  289.4 14.0 %copy-start.3 = (bf16[4096,4,128]{0,2,1:T(8,128)(2,1)S(1)}, bf16[4096,4,128]{0,2,1:T(8,128)(2,1)}, u32[]{:S(2)}) copy-start(bf16[4096,4,128]{0,2,1:T(8,128)(2,1)} %get-tuple-element.114) | copy-start | bytes 12582916 | tf_op jit(solution)/shard_map/cond
  330.5 5.3 %copy-start.1 = (bf16[1,16,8,3584]{3,2,1,0:T(8,128)(2,1)S(1)}, bf16[1,16,8,3584]{3,2,1,0:T(8,128)(2,1)}, u32[]{:S(2)}) copy-start(bf16[1,16,8,3584]{3,2,1,0:T(8,128)(2,1)} %param.14) | copy-start | bytes 2752516
Sparse Core Ops, SparseCore 0:
  49.9 171.1 all-gather.1
